TPU v7x, 32 devices: a whole 2x2x4 slice. The times are simulated.
32 devices in a mesh: shot: 8 (over z, y), xline: 4 (over x, core).
Axes of the slice: x: 2, y: 2, z: 4, core: 2. Of those that a mesh axis runs over, the one named last changes fastest.
Arguments:
- records: bfloat16 [4, 16, 256, 2048], P('xline', 'shot'), may hold values from -1.796875 to 1.796875
- targets: bfloat16 [2048, 32, 256], P('xline', 'shot'), may hold values from -1.796875 to 1.796875
- aperture: int32 [32, 4, 16], P('shot', 'xline'), may hold values from 0 to 255
Outputs:
- multiples: bfloat16 [2048, 32, 256], P('xline', 'shot')
Inputs may be any that keep to these rules, and one draw needn't show every extreme that they name: An aperture entry is the receiver of the output shot at which the contributing source lies.
All inputs are finite; a program needn't handle non-finite values.
Results may differ from a plain program's by a relative error of at most 0.0071.
Values may be sent and summed in bfloat16 or wider, within the bound.
A program may use at most 128 MiB of HBM per device.

v0:
```python
import math
import jax
import jax.numpy as jnp
from jax import lax
from jax.sharding import PartitionSpec as P

NT = 2048
NF = 256


def forward_table():
    times_col = jnp.arange(NT, dtype=jnp.int32)[:, None]
    freq_row = jnp.arange(1, NF + 1, dtype=jnp.int32)[None, :]
    angles = (times_col * freq_row % NT).astype(jnp.float32) * (2.0 * math.pi / NT)
    normalizing_scale = 1.0 / math.sqrt(NT)
    return jnp.concatenate(
        [jnp.cos(angles) * normalizing_scale, -jnp.sin(angles) * normalizing_scale], axis=1
    ).astype(jnp.bfloat16)


def inverse_table():
    times_col = jnp.arange(NT, dtype=jnp.int32)[:, None]
    freq_row = jnp.arange(1, NF + 1, dtype=jnp.int32)[None, :]
    angles = (times_col * freq_row % NT).astype(jnp.float32) * (2.0 * math.pi / NT)
    normalizing_scale = 2.0 / math.sqrt(NT)
    stacked = jnp.stack(
        [jnp.cos(angles) * normalizing_scale, -jnp.sin(angles) * normalizing_scale], axis=2
    )
    return stacked.reshape(NT, 2 * NF)


def complex_mixing(real_part, imag_part):
    upper = jnp.stack([real_part, -imag_part], axis=1)
    lower = jnp.stack([imag_part, real_part], axis=1)
    return jnp.stack([upper, lower], axis=0)


def on_device(records, targets, aperture):
    forward_fourier = forward_table()
    shots_here = targets.shape[1]
    receivers = targets.shape[2]
    gathered = lax.all_gather(targets, "xline", axis=0, tiled=True)
    desired_spectra = jnp.einsum(
        "tsr,tp->srp", gathered, forward_fourier, preferred_element_type=jnp.float32
    ).astype(jnp.bfloat16)
    held = records.shape[1]
    trace_spectra = jnp.einsum(
        "hwn,ne->hew", records[0], forward_fourier, preferred_element_type=jnp.float32
    )
    trace_spectra = trace_spectra.astype(jnp.bfloat16).reshape(held, 2, NF, receivers)
    selects = aperture[:, 0, :]
    receiver_ids = jnp.arange(receivers, dtype=jnp.int32)
    onehot = (selects[:, :, None] == receiver_ids).astype(jnp.bfloat16)
    picked = jnp.einsum(
        "scr,srp->scp", onehot, desired_spectra, preferred_element_type=jnp.float32
    ).astype(jnp.bfloat16)
    mixing = complex_mixing(picked[:, :, :NF], picked[:, :, NF:])
    running = jnp.einsum(
        "qspcf,cpfr->fqsr",
        mixing,
        lax.all_gather(trace_spectra, "shot", axis=0, tiled=True),
        preferred_element_type=jnp.float32,
    )
    inverse_fourier = inverse_table()
    flat_traces = running.reshape(2 * NF, shots_here * receivers)
    time_rows = NT // lax.axis_size("xline")
    summed = lax.psum(flat_traces, "xline")
    inverse_rows = lax.dynamic_slice_in_dim(
        inverse_fourier, lax.axis_index("xline") * time_rows, time_rows, 0
    )
    local_part = jnp.dot(
        inverse_rows, summed, precision=lax.Precision.HIGHEST, preferred_element_type=jnp.float32
    )
    return local_part.reshape(time_rows, shots_here, receivers).astype(jnp.bfloat16)


def solution(mesh):
    in_specs = (P("xline", "shot", None, None), P("xline", "shot", None), P("shot", "xline", None))
    out_specs = P("xline", "shot", None)
    return jax.shard_map(
        on_device, mesh=mesh, in_specs=in_specs, out_specs=out_specs, check_vma=False
    )
```

profile of v0, /device:TPU:0, one launch (start us, length us, event | category | flops | bytes accessed | tf_op | source)
XLA Modules:
  0.0 191.9 jit_solution(8781376290301886159)
XLA Ops:
  6.5 0.0 copy-start
  6.5 0.0 all-gather.3.cloned.1.call-start
  6.5 0.7 all-gather.3.cloned.1.call-update
  7.3 0.0 all-gather.5.cloned.1.call-start
  7.3 9.1 %multiply_convert_fusion.1 = (bf16[2048,256]{0,1:T(8,128)(2,1)S(1)}, bf16[2048,256]{0,1:T(8,128)(2,1)S(1)}) fusion(s32[256]{0:T(256)S(1)} %iota_add_fusion), kind=kLoop, calls=%fused_computation.21 | loop fusion | flops 9961472 | bytes 2098176 | tf_op jit(solution)/shard_map/convert
  16.4 0.0 copy-start.1
  16.4 0.0 copy-done
  16.4 0.0 copy-start.2
  16.4 2.1 %fusion.24 = bf16[512,2,256]{2,0,1:T(8,128)(2,1)} fusion(bf16[1,2,256,2048]{3,2,1,0:T(8,128)(2,1)S(1)} %copy-done, bf16[2048,256]{0,1:T(8,128)(2,1)S(1)} %get-tuple-element.13, bf16[2048,256]{0,1:T(8,128)(2,1)S(1)} %get-tuple-element.12), kind=kOutput, calls=%fused_computation.33 | convolution fusion | flops 1078198272 | bytes 4718592 | tf_op jit(solution)/shard_map/hwn,ne->hew/dot_general | solution.py:47
  18.6 0.0 copy-done.1
  18.6 0.0 all-gather.5.cloned.1.call-update
  18.6 0.0 all-reduce.2.cloned.1.call-start
  18.6 27.5 %all-gather.3.cloned.1.call-done = bf16[2048,4,256]{2,1,0:T(4,128)(2,1)} async-done(((bf16[512,4,256]{2,1,0:T(4,128)(2,1)}), bf16[2048,4,256]{2,1,0:T(4,128)(2,1)}) %all-gather.3.cloned.1.call-update) | async-done | bytes 4194320 | tf_op jit(solution)/shard_map/all_gather | solution.py:42
  46.2 0.0 copy-done.2
  46.2 5.0 %fusion.30 = bf16[4,16,512]{2,1,0:T(8,128)(2,1)S(1)} fusion(bf16[2048,4,256]{2,1,0:T(4,128)(2,1)} %all-gather.3.cloned.1.call-done, bf16[2048,256]{0,1:T(8,128)(2,1)} %copy-done.1, bf16[2048,256]{0,1:T(8,128)(2,1)S(1)} %get-tuple-element.12, s32[4,16]{1,0:T(4,128)S(1)} %bitcast.49), kind=kOutput, calls=%fused_computation.35 | convolution fusion | flops 2169028608 | bytes 6357248 | tf_op jit(solution)/shard_map/scr,srp->scp/dot_general | solution.py:54
  51.3 1.1 copy.15
  52.4 68.8 %all-gather.5.cloned.1.call-done = bf16[16,2,256,256]{3,2,1,0:T(8,128)(2,1)} async-done(((bf16[2,2,256,256]{3,2,1,0:T(8,128)(2,1)}), bf16[16,2,256,256]{3,2,1,0:T(8,128)(2,1)}) %all-gather.5.cloned.1.call-update) | async-done | bytes 4194320 | tf_op jit(solution)/shard_map/all_gather | solution.py:61
  121.2 5.3 %fusion = f32[256,2,4,256,1]{3,2,4,1,0:T(4,128)S(1)} fusion(bf16[2,4,2,16,256]{3,1,2,0,4:T(4,128)(2,1)S(1)} %copy.15, bf16[16,2,256,256,1]{3,2,1,0,4:T(8,128)(2,1)} %bitcast.47), kind=kOutput, calls=%fused_computation.1 | convolution fusion | flops 33554432 | bytes 6422528 | tf_op jit(solution)/shard_map/qspcf,cpfr->fqsr/dot_general | solution.py:58
  126.5 1.8 copy.22
  128.3 0.0 all-reduce.2.cloned.1.call-update
  128.3 8.5 %cosine_multiply_fusion = (f32[2048,256,1]{1,0,2:T(8,128)S(1)}, f32[2048,256,1]{1,0,2:T(8,128)S(1)}) fusion(s32[256]{0:T(256)S(1)} %iota_add_fusion), kind=kLoop, calls=%fused_computation.25 | loop fusion | flops 8912896 | bytes 4195328 | tf_op jit(solution)/shard_map/mul | solution.py:27
  136.9 2.2 %pad_maximum_fusion = f32[2048,256,2]{1,0,2:T(8,128)} fusion(f32[2048,256,1]{1,0,2:T(8,128)S(1)} %get-tuple-element.11, f32[2048,256,1]{1,0,2:T(8,128)S(1)} %get-tuple-element.10), kind=kLoop, calls=%fused_computation | loop fusion | flops 1048576 | bytes 8388608 | tf_op jit(solution)/shard_map/stack | solution.py:26
  139.1 7.4 %copy.12 = f32[2048,256,2]{0,2,1:T(2,128)} copy(f32[2048,256,2]{1,0,2:T(8,128)} %pad_maximum_fusion) | data formatting | bytes 8388608 | tf_op jit(solution)/shard_map/stack | solution.py:26
  146.5 6.1 %reshape.122 = f32[2048,512]{0,1:T(8,128)} reshape(f32[2048,256,2]{0,2,1:T(2,128)} %copy.12) | data formatting | bytes 8388608 | tf_op jit(solution)/shard_map/reshape | solution.py:29
  152.6 25.8 %all-reduce.2.cloned.1.call-done = f32[512,1024]{1,0:T(8,128)} async-done(((f32[512,1024]{1,0:T(8,128)}), f32[512,1024]{1,0:T(8,128)}) %all-reduce.2.cloned.1.call-update) | async-done | bytes 2097168 | tf_op jit(solution)/shard_map/psum | solution.py:67
  178.4 5.4 %convolution_convert_fusion = bf16[512,1024]{1,0:T(8,128)(2,1)S(1)} fusion(f32[512,1024]{1,0:T(8,128)} %all-reduce.2.cloned.1.call-done, f32[2048,512]{0,1:T(8,128)} %reshape.122, s32[]{:T(128)S(6)} %select_n.30), kind=kOutput, calls=%fused_computation.30 | convolution fusion | flops 3221749760 | bytes 4194308 | tf_op jit(solution)/shard_map/dot_general | solution.py:71
  183.8 1.6 convert_element_type.52
  (4 shorter events, 0.1 us)
Async XLA Ops:
  6.5 9.9 %copy-start = (bf16[1,2,256,2048]{3,2,1,0:T(8,128)(2,1)S(1)}, bf16[1,2,256,2048]{3,2,1,0:T(8,128)(2,1)}, u32[]{:S(2)}) copy-start(bf16[1,2,256,2048]{3,2,1,0:T(8,128)(2,1)} %param.3) | copy-start | bytes 6291460
  6.5 39.6 %all-gather.3.cloned.1.call-start = ((), (), s32[]{:S(2)}) async-start(), calls=%async_computation | async-start | bytes 5242880 | tf_op jit(solution)/shard_map/all_gather | solution.py:42
  7.3 113.9 %all-gather.5.cloned.1.call-start = ((), (), s32[]{:S(2)}) async-start(), calls=%async_computation.1 | async-start | bytes 4718592 | tf_op jit(solution)/shard_map/all_gather | solution.py:61
  16.4 2.2 %copy-start.1 = (bf16[2048,256]{0,1:T(8,128)(2,1)}, bf16[2048,256]{0,1:T(8,128)(2,1)S(1)}, u32[]{:S(2)}) copy-start(bf16[2048,256]{0,1:T(8,128)(2,1)S(1)} %get-tuple-element.13) | copy-start | bytes 3145732
  16.4 29.8 %copy-start.2 = (s32[4,1,16]{2,1,0:T(1,128)S(1)}, s32[4,1,16]{2,1,0:T(1,128)}, u32[]{:S(2)}) copy-start(s32[4,1,16]{2,1,0:T(1,128)} %param.5) | copy-start | bytes 772
  18.6 159.8 %all-reduce.2.cloned.1.call-start = ((), (), s32[]{:S(2)}) async-start(), calls=%async_computation.2 | async-start | bytes 4194304 | tf_op jit(solution)/shard_map/psum | solution.py:67
Sparse Core Ops, SparseCore 0:
  8.9 37.2 all-gather.2
  48.3 72.8 all-gather.4
  128.4 49.9 all-reduce.1
where the time goes:
time: 192 us
  waiting for transfers between devices  123 us (64%)
  other arithmetic  19.9 us (10%)
  local copies, waits for them, and re-layouts  18 us (9%)
  matrix products  17.9 us (9%)
  between operations  13.2 us (7%)
    all_gather x1, waiting for transfers between devices, on_device(): lax.all_gather(trace_spectra, 'shot', axis=0, tiled=True)  68.8 us
    all_gather x1, waiting for transfers between devices, on_device(): gathered = lax.all_gather(targets, 'xline', axis=0, tiled=True)  27.5 us
    psum x1, waiting for transfers between devices, on_device(): summed = lax.psum(flat_traces, 'xline')  25.8 us
    another operation x1, other arithmetic  9.05 us
    mul x1, other arithmetic, inverse_table(): jnp.cos(angles) * normalizing_scale  8.53 us
    another operation x1, local copies, waits for them, and re-layouts, inverse_table(): jnp.stack([jnp.cos(angles) * normalizing_scale, -jnp.sin(angles) * normal...  7.43 us
    reshape x1, local copies, waits for them, and re-layouts, inverse_table(): return stacked.reshape(NT, 2 * NF)  6.09 us
    dot_general x1, matrix products, on_device(): jnp.dot(inverse_rows, summed, precision=lax.Precision.HIGHEST, preferred_...  5.4 us
  transfers between devices with their start and end apart: 3, of which 3 were waited for; matrix products, arithmetic and copies ran while one was open for 22% of the time, Pallas kernels for 0%

commit v1 on v0

--- a/solution.py
+++ b/solution.py
@@ -64,7 +64,7 @@
     inverse_fourier = inverse_table()
     flat_traces = running.reshape(2 * NF, shots_here * receivers)
     time_rows = NT // lax.axis_size("xline")
-    summed = lax.psum(flat_traces, "xline")
+    summed = jnp.sum(lax.all_gather(flat_traces, "xline"), axis=0)
     inverse_rows = lax.dynamic_slice_in_dim(
         inverse_fourier, lax.axis_index("xline") * time_rows, time_rows, 0
     )

time: 192 us -> 214 us (1.11)
  waiting for transfers between devices: 123 us -> 130 us
  other arithmetic: 19.9 us -> 26.2 us
  matrix products: 17.9 us -> 22.5 us
  local copies, waits for them, and re-layouts: 18 us -> 22.4 us
    all_gather x0 -> x1, waiting for transfers between devices: none -> 32.3 us  [on_device(): summed = jnp.sum(lax.all_gather(flat_traces, 'xline'), axis=0)]
    psum x1 -> x0, waiting for transfers between devices: 25.8 us -> none  [on_device(): summed = lax.psum(flat_traces, 'xline')]
    reduce_sum x0 -> x1, other arithmetic: none -> 5.9 us  [on_device(): summed = jnp.sum(lax.all_gather(flat_traces, 'xline'), axis=0)]
    another operation x0 -> x1, local copies, waits for them, and re-layouts: none -> 3.32 us  [on_device(): summed = jnp.sum(lax.all_gather(flat_traces, 'xline'), axis=0)]
    dot_general x1, matrix products: 5.4 us -> 8.63 us  [on_device(): jnp.dot(inverse_rows, summed, precision=lax.Precision.HIGHEST, preferred_...]
    dot_general x0 -> x1, local copies, waits for them, and re-layouts: none -> 2.91 us  [on_device(): jnp.dot(inverse_rows, summed, precision=lax.Precision.HIGHEST, preferred_...]
  transfers between devices with their start and end apart: 3 -> 3, of which waited for: 3 -> 3; matrix products, arithmetic and copies ran while one was open for 22% -> 20% of each run, Pallas kernels for 0% -> 0%
where the time goes in v1:
time: 214 us
  waiting for transfers between devices  130 us (61%)
  other arithmetic  26.2 us (12%)
  matrix products  22.5 us (11%)
  local copies, waits for them, and re-layouts  22.4 us (10%)
  between operations  13.2 us (6%)
    all_gather x1, waiting for transfers between devices, on_device(): lax.all_gather(trace_spectra, 'shot', axis=0, tiled=True)  68.9 us
    all_gather x1, waiting for transfers between devices, on_device(): summed = jnp.sum(lax.all_gather(flat_traces, 'xline'), axis=0)  32.3 us
    all_gather x1, waiting for transfers between devices, on_device(): gathered = lax.all_gather(targets, 'xline', axis=0, tiled=True)  27.5 us
    another operation x1, other arithmetic  9.05 us
    dot_general x1, matrix products, on_device(): jnp.dot(inverse_rows, summed, precision=lax.Precision.HIGHEST, preferred_...  8.63 us
    mul x1, other arithmetic, inverse_table(): jnp.cos(angles) * normalizing_scale  8.31 us
    another operation x1, local copies, waits for them, and re-layouts, inverse_table(): jnp.stack([jnp.cos(angles) * normalizing_scale, -jnp.sin(angles) * normal...  7.42 us
    dot_general x1, matrix products, on_device(): jnp.einsum('qspcf,cpfr->fqsr', mixing, lax.all_gather(trace_spectra, 'sho...  6.68 us
  transfers between devices with their start and end apart: 3, of which 3 were waited for; matrix products, arithmetic and copies ran while one was open for 20% of the time, Pallas kernels for 0%

profile of v1, /device:TPU:0, one launch (start us, length us, event | category | flops | bytes accessed | tf_op | source)
XLA Modules:
  0.0 213.9 jit_solution(6634790961960913567)
XLA Ops:
  6.5 0.0 copy-start
  6.5 0.0 all-gather.4.cloned.1.call-start
  6.5 0.7 all-gather.4.cloned.1.call-update
  7.3 0.0 all-gather.6.cloned.1.call-start
  7.3 9.1 %multiply_convert_fusion.1 = (bf16[2048,256]{0,1:T(8,128)(2,1)S(1)}, bf16[2048,256]{0,1:T(8,128)(2,1)S(1)}) fusion(s32[256]{0:T(256)S(1)} %iota_add_fusion), kind=kLoop, calls=%fused_computation.21 | loop fusion | flops 9961472 | bytes 2098176 | tf_op jit(solution)/shard_map/convert
  16.4 0.0 copy-start.1
  16.4 0.0 copy-done
  16.4 0.0 copy-start.2
  16.4 2.1 %fusion.27 = bf16[512,2,256]{2,0,1:T(8,128)(2,1)} fusion(bf16[1,2,256,2048]{3,2,1,0:T(8,128)(2,1)S(1)} %copy-done, bf16[2048,256]{0,1:T(8,128)(2,1)S(1)} %get-tuple-element.13, bf16[2048,256]{0,1:T(8,128)(2,1)S(1)} %get-tuple-element.12), kind=kOutput, calls=%fused_computation.34 | convolution fusion | flops 1078198272 | bytes 4718592 | tf_op jit(solution)/shard_map/hwn,ne->hew/dot_general | solution.py:47
  18.6 0.0 copy-done.1
  18.6 0.0 all-gather.6.cloned.1.call-update
  18.6 0.0 all-gather.8.cloned.1.call-start
  18.6 27.5 %all-gather.4.cloned.1.call-done = bf16[2048,4,256]{2,1,0:T(4,128)(2,1)} async-done(((bf16[512,4,256]{2,1,0:T(4,128)(2,1)}), bf16[2048,4,256]{2,1,0:T(4,128)(2,1)}) %all-gather.4.cloned.1.call-update) | async-done | bytes 4194320 | tf_op jit(solution)/shard_map/all_gather | solution.py:42
  46.2 0.0 copy-done.2
  46.2 5.0 %fusion.33 = bf16[4,16,512]{2,1,0:T(8,128)(2,1)S(1)} fusion(bf16[2048,4,256]{2,1,0:T(4,128)(2,1)} %all-gather.4.cloned.1.call-done, bf16[2048,256]{0,1:T(8,128)(2,1)} %copy-done.1, bf16[2048,256]{0,1:T(8,128)(2,1)S(1)} %get-tuple-element.12, s32[4,16]{1,0:T(4,128)S(1)} %bitcast.53), kind=kOutput, calls=%fused_computation.36 | convolution fusion | flops 2169028608 | bytes 6357248 | tf_op jit(solution)/shard_map/scr,srp->scp/dot_general | solution.py:54
  51.3 0.9 copy.22
  52.2 68.9 %all-gather.6.cloned.1.call-done = bf16[16,2,256,256]{3,2,1,0:T(8,128)(2,1)} async-done(((bf16[2,2,256,256]{3,2,1,0:T(8,128)(2,1)}), bf16[16,2,256,256]{3,2,1,0:T(8,128)(2,1)}) %all-gather.6.cloned.1.call-update) | async-done | bytes 4194320 | tf_op jit(solution)/shard_map/all_gather | solution.py:61
  121.2 6.7 %fusion.18 = f32[256,2,4,256]{3,2,1,0:T(4,128)} fusion(bf16[2,4,2,16,256]{3,1,2,0,4:T(4,128)(2,1)S(1)} %copy.22, bf16[16,2,256,256,1]{3,2,1,0,4:T(8,128)(2,1)} %bitcast.51), kind=kOutput, calls=%fused_computation.30 | convolution fusion | flops 33554432 | bytes 6422528 | tf_op jit(solution)/shard_map/qspcf,cpfr->fqsr/dot_general | solution.py:58
  127.8 3.3 %all_gather_reshape.3 = f32[1,512,1024]{2,1,0:T(8,128)} reshape(f32[256,2,4,256]{3,2,1,0:T(4,128)} %fusion.18) | data formatting | bytes 4194304 | tf_op jit(solution)/shard_map/all_gather;reshape | solution.py:67
  131.2 0.0 all-gather.8.cloned.1.call-update
  131.2 8.3 %cosine_multiply_fusion = (f32[2048,256,1]{1,0,2:T(8,128)S(1)}, f32[2048,256,1]{1,0,2:T(8,128)S(1)}) fusion(s32[256]{0:T(256)S(1)} %iota_add_fusion), kind=kLoop, calls=%fused_computation.25 | loop fusion | flops 8912896 | bytes 4195328 | tf_op jit(solution)/shard_map/mul | solution.py:27
  139.5 2.9 %pad_maximum_fusion = f32[2048,256,2]{1,0,2:T(8,128)} fusion(f32[2048,256,1]{1,0,2:T(8,128)S(1)} %get-tuple-element.11, f32[2048,256,1]{1,0,2:T(8,128)S(1)} %get-tuple-element.10), kind=kLoop, calls=%fused_computation | loop fusion | flops 1048576 | bytes 8388608 | tf_op jit(solution)/shard_map/stack | solution.py:26
  142.4 7.4 %copy.18 = f32[2048,256,2]{0,2,1:T(2,128)} copy(f32[2048,256,2]{1,0,2:T(8,128)} %pad_maximum_fusion) | data formatting | bytes 8388608 | tf_op jit(solution)/shard_map/stack | solution.py:26
  149.8 6.1 %reshape.119 = f32[2048,512]{0,1:T(8,128)} reshape(f32[2048,256,2]{0,2,1:T(2,128)} %copy.18) | data formatting | bytes 8388608 | tf_op jit(solution)/shard_map/reshape | solution.py:29
  155.9 32.3 %all-gather.8.cloned.1.call-done = f32[4,512,1024]{2,1,0:T(8,128)} async-done(((f32[1,512,1024]{2,1,0:T(8,128)}), f32[4,512,1024]{2,1,0:T(8,128)}) %all-gather.8.cloned.1.call-update) | async-done | bytes 8388624 | tf_op jit(solution)/shard_map/all_gather | solution.py:67
  188.1 5.9 %reduce_sum.9 = f32[512,1024]{1,0:T(8,128)} reduce(f32[4,512,1024]{2,1,0:T(8,128)} %all-gather.8.cloned.1.call-done, f32[]{:T(128)} %constant.36.clone.1), dimensions={0}, to_apply=%region_0.1 | reduce | flops 1572864 | bytes 10485764 | tf_op jit(solution)/shard_map/reduce_sum | solution.py:67
  194.0 2.9 %copy.31 = f32[1024,512]{1,0:T(8,128)} copy(f32[1024,512]{0,1:T(8,128)} %bitcast.50) | data formatting | bytes 4194304 | tf_op jit(solution)/shard_map/dot_general | solution.py:71
  196.9 8.6 %convolution_convert_fusion = bf16[512,4,256]{2,0,1:T(8,128)(2,1)S(1)} fusion(f32[4,256,512]{2,1,0:T(8,128)} %bitcast.49, f32[2048,512]{0,1:T(8,128)} %reshape.119, s32[]{:T(128)S(6)} %select_n.30), kind=kOutput, calls=%fused_computation.31 | convolution fusion | flops 3221749760 | bytes 4194308 | tf_op jit(solution)/shard_map/dot_general | solution.py:71
  205.6 1.8 copy.25
  (4 shorter events, 0.1 us)
Async XLA Ops:
  6.5 9.9 %copy-start = (bf16[1,2,256,2048]{3,2,1,0:T(8,128)(2,1)S(1)}, bf16[1,2,256,2048]{3,2,1,0:T(8,128)(2,1)}, u32[]{:S(2)}) copy-start(bf16[1,2,256,2048]{3,2,1,0:T(8,128)(2,1)} %param.3) | copy-start | bytes 6291460
  6.5 39.6 %all-gather.4.cloned.1.call-start = ((), (), s32[]{:S(2)}) async-start(), calls=%async_computation | async-start | bytes 5242880 | tf_op jit(solution)/shard_map/all_gather | solution.py:42
  7.3 113.9 %all-gather.6.cloned.1.call-start = ((), (), s32[]{:S(2)}) async-start(), calls=%async_computation.1 | async-start | bytes 4718592 | tf_op jit(solution)/shard_map/all_gather | solution.py:61
  16.4 2.2 %copy-start.1 = (bf16[2048,256]{0,1:T(8,128)(2,1)}, bf16[2048,256]{0,1:T(8,128)(2,1)S(1)}, u32[]{:S(2)}) copy-start(bf16[2048,256]{0,1:T(8,128)(2,1)S(1)} %get-tuple-element.13) | copy-start | bytes 3145732
  16.4 29.8 %copy-start.2 = (s32[4,1,16]{2,1,0:T(1,128)S(1)}, s32[4,1,16]{2,1,0:T(1,128)}, u32[]{:S(2)}) copy-start(s32[4,1,16]{2,1,0:T(1,128)} %param.5) | copy-start | bytes 772
  18.6 169.6 %all-gather.8.cloned.1.call-start = ((), (), s32[]{:S(2)}) async-start(), calls=%async_computation.2 | async-start | bytes 10485760 | tf_op jit(solution)/shard_map/all_gather | solution.py:67
Sparse Core Ops, SparseCore 0:
  8.9 37.2 all-gather.3
  48.3 72.8 all-gather.5
  131.3 56.7 all-gather.7
